TPU v7x, 32 devices: a whole 2x2x4 slice. The times are simulated.
32 devices in a mesh: groups: 2 (over y), owners: 4 (over z), section: 2 (over x), rep: 2 (over core).
Axes of the slice: x: 2, y: 2, z: 4, core: 2. Of those that a mesh axis runs over, the one named last changes fastest.
Arguments:
- inputs: bfloat16 [2, 4096, 512], P('section', 'owners', ('groups', 'rep')), parts along dimension 2, may hold values from -6 to 6
- weight_first: bfloat16 [2, 32, 2048, 128], P('section', ('owners', 'rep')), may hold values from -0.1875 to 0.1875
- weight_second: bfloat16 [2, 32, 1024, 128], P('section', ('owners', 'rep')), may hold values from -0.25 to 0.25
- bias_first: float32 [2, 4096], P('section', 'owners'), may hold values from -1.5 to 1.5
- bias_second: float32 [2, 4096], P('section', 'owners'), may hold values from -1.5 to 1.5
- links_first: int32 [2, 32, 16], P('section', 'owners'), may hold values from 0 to 15, as said below
- links_second: int32 [2, 32, 8], P('section', 'owners'), may hold values from 0 to 7, as said below
Outputs:
- final_activity: bfloat16 [2, 4096, 512], P('section', 'owners', ('groups', 'rep')), parts along dimension 2
There are 2 independent parts, one for each index of `groups`. A program takes and returns all parts, laid end to end along the dimension named above; an argument that names none is the same for every part. Nothing has to cross between parts.
Inputs may be any that keep to these rules, and one draw needn't show every extreme that they name: `links_first`: in every row of every section the 16 entries are distinct. `links_second`: in every row of every section the 8 entries are distinct.
All inputs are finite; a program needn't handle non-finite values.
Results may differ from a plain program's by a relative error of at most 0.014.
Values may be sent and summed in bfloat16 or wider, within the bound.
A program may use at most 64 MiB of HBM per device.

v0:
```python
import jax
import jax.numpy as jnp
from jax import lax
from jax.sharding import PartitionSpec as P

CEILING = 4.0


def from_behind(value, axis, steps):
    count = lax.axis_size(axis)
    pairs = [(source, (source + steps) % count) for source in range(count)]
    return lax.ppermute(value, axis, pairs)


def swapped(block, axis, distance):
    count = lax.axis_size(axis)
    route = []
    for low in range(count):
        high = low | 1 << distance
        if high != low and high < count:
            route += [(low, high), (high, low)]
    return lax.ppermute(block, axis, route)


def passed_along(array, axis, by):
    size = lax.axis_size(axis)
    pairs = [(i, i + by) for i in range(size) if 0 <= i + by < size]
    return lax.ppermute(array, axis, pairs)


def order_tiles(tiles, link_table):
    block_count = tiles.shape[0]
    radix_len = link_table.shape[1]
    tile_size = tiles.shape[2]
    inverse = jnp.argsort(link_table, axis=1)
    shaped = tiles.reshape(block_count, radix_len, tile_size, tile_size)
    ordered = jnp.take_along_axis(shaped, inverse[:, :, None, None], axis=1)
    return ordered.reshape(block_count, radix_len * tile_size, tile_size)


def mixed_layer(group_rows, ordered, bias_row):
    block_count = ordered.shape[0]
    tile_size = ordered.shape[2]
    row_count = group_rows.shape[1]
    summed = jnp.einsum("bkc,kr->bcr", ordered, group_rows, preferred_element_type=jnp.float32)
    summed = summed.reshape(block_count * tile_size, row_count) + bias_row[:, None]
    return jnp.clip(summed, 0.0, CEILING).astype(jnp.bfloat16)


def rotate_slots(slot_store):
    return from_behind(slot_store, "section", 1)


def body(inputs, weight_first, weight_second, bias_first, bias_second, links_first, links_second):
    section_count = lax.axis_size("section")
    section_here = lax.axis_index("section")
    owner_parity = lax.axis_index("owners") % 2
    slot_store = inputs[0]
    row_count = slot_store.shape[1]
    owner_width = slot_store.shape[0]
    zeros_own = jnp.zeros((owner_width, row_count), jnp.bfloat16)
    full_first, full_second = (
        lax.all_gather(weight_first, "rep", axis=1, tiled=True),
        lax.all_gather(weight_second, "rep", axis=1, tiled=True),
    )
    first_tiles = order_tiles(full_first[0], links_first[0])
    second_tiles = order_tiles(full_second[0], links_second[0])
    handed = zeros_own
    tick_total = 2 * section_count - 1
    for tick_index in range(tick_total):
        if tick_index < section_count:
            incoming = jnp.where(section_here == 0, slot_store, handed)
        else:
            incoming = handed
        active = jnp.logical_and(
            section_here <= tick_index, section_here > tick_index - section_count
        )
        own_half = lax.all_to_all(incoming, "owners", split_axis=0, concat_axis=0, tiled=True)
        other_half = swapped(own_half, "owners", 0)
        lower_half = jnp.where(owner_parity == 0, own_half, other_half)
        upper_half = jnp.where(owner_parity == 0, other_half, own_half)
        apply_group_rows = jnp.concatenate([lower_half, upper_half], axis=0)
        middle = lax.cond(
            active,
            lambda: mixed_layer(apply_group_rows, first_tiles, bias_first[0]),
            lambda: zeros_own,
        )
        regrouped = lax.all_to_all(middle, "owners", split_axis=0, concat_axis=0, tiled=True)
        group_rows = regrouped
        result = lax.cond(
            active, lambda: mixed_layer(group_rows, second_tiles, bias_second[0]), lambda: zeros_own
        )
        if tick_index >= section_count - 1:
            slot_store = jnp.where(section_here == section_count - 1, result, slot_store)
        if tick_index < tick_total - 1:
            handed = passed_along(result, "section", 1)
        slot_store = rotate_slots(slot_store)
    slot_store = rotate_slots(slot_store)
    return slot_store[None]


def solution(mesh):
    placed = (
        P("section", "owners", ("groups", "rep")),
        P("section", ("owners", "rep"), None, None),
        P("section", ("owners", "rep"), None, None),
        P("section", "owners"),
        P("section", "owners"),
        P("section", "owners", None),
        P("section", "owners", None),
    )
    return jax.shard_map(
        body,
        mesh=mesh,
        in_specs=placed,
        out_specs=P("section", "owners", ("groups", "rep")),
        check_vma=False,
    )
```

profile of v0, /device:TPU:6, one launch (start us, length us, event | category | flops | bytes accessed | tf_op | source)
XLA Modules:
  0.0 173.7 jit_solution(9513110891252928978)
XLA Ops:
  8.2 4.9 %all-to-all-start = ((bf16[4,256,128]{2,1,0:T(8,128)(2,1)}), bf16[4,256,128]{2,1,0:T(8,128)(2,1)S(1)}, u32[]{:S(2)}, u32[]{:S(2)}) async-start(bf16[4,256,128]{2,1,0:T(8,128)(2,1)} %bitcast.34), calls=%async_computation | async-start | bytes 524288 | tf_op jit(solution)/shard_map/all_to_all | solution.py:78
  15.5 6.5 %all-to-all-done = bf16[4,256,128]{2,1,0:T(8,128)(2,1)S(1)} async-done(((bf16[4,256,128]{2,1,0:T(8,128)(2,1)}), bf16[4,256,128]{2,1,0:T(8,128)(2,1)S(1)}, u32[]{:S(2)}, u32[]{:S(2)}) %all-to-all-start) | async-done | bytes 262176 | tf_op jit(solution)/shard_map/all_to_all | solution.py:78
  22.4 6.0 %collective-permute-done.1 = bf16[1024,128]{1,0:T(8,128)(2,1)S(1)} collective-permute-done((bf16[1024,128]{1,0:T(8,128)(2,1)S(1)}, bf16[1024,128]{1,0:T(8,128)(2,1)S(1)}, u32[]{:S(2)}, u32[]{:S(2)}) %collective-permute-start.1) | collective-permute-done | bytes 262176 | tf_op jit(solution)/shard_map/ppermute | solution.py:22
  28.5 5.3 %gather_fusion.1 = bf16[128,128,128]{2,1,0:T(8,128)(2,1)} fusion(bf16[8,16,128,128]{3,2,1,0:T(8,128)(2,1)} %bitcast.97, s32[128]{0:T(128)S(1)} %reshape.94), kind=kCustom, calls=%fused_computation.1 | custom fusion | bytes 8389632 | tf_op jit(solution)/shard_map/jit(take_along_axis)/gather | solution.py:37
  33.9 7.8 %bitcast_select_fusion = bf16[8,2048,128]{2,1,0:T(8,128)(2,1)} fusion(pred[8,2048]{1,0:T(8,128)(4,1)S(1)} %broadcast_bitcast_fusion, bf16[8,2048,128]{2,1,0:T(8,128)(2,1)} %bitcast.95), kind=kLoop, calls=%fused_computation.26 | loop fusion | flops 2097152 | bytes 8404992 | tf_op jit(solution)/shard_map/jit(take_along_axis)/select_n | solution.py:37
  42.4 3.7 %all-to-all-start.1 = ((bf16[4,256,128]{2,1,0:T(8,128)(2,1)}), bf16[4,256,128]{2,1,0:T(8,128)(2,1)S(1)}, u32[]{:S(2)}, u32[]{:S(2)}) async-start(bf16[4,256,128]{2,1,0:T(8,128)(2,1)} %bitcast.36), calls=%async_computation.1 | async-start | bytes 524288 | tf_op jit(solution)/shard_map/all_to_all | solution.py:88
  46.2 3.8 %gather_fusion = bf16[64,128,128]{2,1,0:T(8,128)(2,1)} fusion(bf16[8,8,128,128]{3,2,1,0:T(8,128)(2,1)} %bitcast.99, s32[64]{0:T(128)S(1)} %reshape.88), kind=kCustom, calls=%fused_computation | custom fusion | bytes 4194816 | tf_op jit(solution)/shard_map/jit(take_along_axis)/gather | solution.py:37
  50.0 4.8 %bitcast_select_fusion.1 = bf16[8,1024,128]{2,1,0:T(8,128)(2,1)S(1)} fusion(pred[8,1024]{1,0:T(8,128)(4,1)S(1)} %broadcast_bitcast_fusion.1, bf16[8,1024,128]{2,1,0:T(8,128)(2,1)} %bitcast.96), kind=kLoop, calls=%fused_computation.27 | loop fusion | flops 1048576 | bytes 4202496 | tf_op jit(solution)/shard_map/jit(take_along_axis)/select_n | solution.py:37
  56.2 13.4 %collective-permute-done.2 = bf16[1024,128]{1,0:T(8,128)(2,1)S(1)} collective-permute-done((bf16[1024,128]{1,0:T(8,128)(2,1)S(1)}, bf16[1024,128]{1,0:T(8,128)(2,1)S(1)}, u32[]{:S(2)}, u32[]{:S(2)}) %collective-permute-start.2) | collective-permute-done | bytes 262176 | tf_op jit(solution)/shard_map/ppermute | solution.py:28
  69.6 13.3 %all_to_all.66 = bf16[4,256,128]{2,1,0:T(8,128)(2,1)S(1)} all-to-all(bf16[4,256,128]{2,1,0:T(8,128)(2,1)S(1)} %bitcast.107), channel_id=1, replica_groups=mesh['groups'=2,'owners'=4,'section'=2,'rep'=2] {'owners'}, dimensions={0} | all-to-all | bytes 524288 | tf_op jit(solution)/shard_map/all_to_all | solution.py:78
  84.9 4.4 %collective-permute-done.3 = bf16[1024,128]{1,0:T(8,128)(2,1)S(1)} collective-permute-done((bf16[1024,128]{1,0:T(8,128)(2,1)S(1)}, bf16[1024,128]{1,0:T(8,128)(2,1)S(1)}, u32[]{:S(2)}, u32[]{:S(2)}) %collective-permute-start.3) | collective-permute-done | bytes 262176 | tf_op jit(solution)/shard_map/ppermute | solution.py:22
  89.4 4.4 %conditional.8 = (bf16[1024,128]{1,0:T(8,128)(2,1)}) conditional(s32[]{:T(128)} %convert_element_type.31, () %tuple.44, (bf16[8,2048,128]{2,1,0:T(8,128)(2,1)}, bf16[2048,128]{1,0:T(8,128)(2,1)S(1)}, f32[1,1024]{1,0:T(1,128)S(1)}) %tuple.88), branch_computations={%region_6.7_spmd, %region_7.8_spmd} | conditional | flops 537264128 | bytes 6033416 | solution.py:83
  89.4 3.5 %fusion.8 = f32[8,128,128]{2,1,0:T(8,128)S(1)} fusion(bf16[8,2048,128]{2,1,0:T(8,128)(2,1)} %get-tuple-element.117, bf16[2048,128]{1,0:T(8,128)(2,1)S(1)} %get-tuple-element.69), kind=kOutput, calls=%fused_computation.13 | convolution fusion | flops 536870912 | bytes 5242880 | tf_op jit(solution)/shard_map/cond/branch_1_fun/bkc,kr->bcr/dot_general | solution.py:45
  97.2 6.7 %all-to-all-done.3 = bf16[4,256,128]{2,1,0:T(8,128)(2,1)S(1)} async-done(((bf16[4,256,128]{2,1,0:T(8,128)(2,1)}), bf16[4,256,128]{2,1,0:T(8,128)(2,1)S(1)}, u32[]{:S(2)}, u32[]{:S(2)}) %all-to-all-start.3) | async-done | bytes 262176 | tf_op jit(solution)/shard_map/all_to_all | solution.py:88
  103.9 4.9 %conditional.9 = (bf16[1024,128]{1,0:T(8,128)(2,1)S(1)}) conditional(s32[]{:T(128)} %convert_element_type.31, () %tuple.43, (bf16[8,1024,128]{2,1,0:T(8,128)(2,1)S(1)}, bf16[4,256,128]{2,1,0:T(8,128)(2,1)S(1)}, f32[1,1024]{1,0:T(1,128)S(1)}) %tuple.91), branch_computations={%region_8.9_spmd, %region_9.10_spmd} | conditional | flops 268828672 | bytes 6819848 | solution.py:90
  110.1 7.0 %collective-permute-done.4 = bf16[1024,128]{1,0:T(8,128)(2,1)S(1)} collective-permute-done((bf16[1024,128]{1,0:T(8,128)(2,1)S(1)}, bf16[1024,128]{1,0:T(8,128)(2,1)S(1)}, u32[]{:S(2)}, u32[]{:S(2)}) %collective-permute-start.4) | collective-permute-done | bytes 262176 | tf_op jit(solution)/shard_map/ppermute | solution.py:28
  117.1 10.4 %all_to_all.67 = bf16[4,256,128]{2,1,0:T(8,128)(2,1)S(1)} all-to-all(bf16[4,256,128]{2,1,0:T(8,128)(2,1)S(1)} %bitcast.113), channel_id=1, replica_groups=mesh['groups'=2,'owners'=4,'section'=2,'rep'=2] {'owners'}, dimensions={0} | all-to-all | bytes 524288 | tf_op jit(solution)/shard_map/all_to_all | solution.py:78
  128.5 5.3 %collective-permute-done.5 = bf16[1024,128]{1,0:T(8,128)(2,1)S(1)} collective-permute-done((bf16[1024,128]{1,0:T(8,128)(2,1)S(1)}, bf16[1024,128]{1,0:T(8,128)(2,1)S(1)}, u32[]{:S(2)}, u32[]{:S(2)}) %collective-permute-start.5) | collective-permute-done | bytes 262176 | tf_op jit(solution)/shard_map/ppermute | solution.py:22
  133.9 4.4 %conditional.10 = (bf16[1024,128]{1,0:T(8,128)(2,1)}) conditional(s32[]{:T(128)} %convert_element_type.30, () %tuple.42, (bf16[8,2048,128]{2,1,0:T(8,128)(2,1)}, bf16[2048,128]{1,0:T(8,128)(2,1)S(1)}, f32[1,1024]{1,0:T(1,128)S(1)}) %tuple.89), branch_computations={%region_10.11_spmd, %region_11.12_spmd} | conditional | flops 537264128 | bytes 6033416 | solution.py:83
  133.9 3.5 %fusion.14 = f32[8,128,128]{2,1,0:T(8,128)S(1)} fusion(bf16[8,2048,128]{2,1,0:T(8,128)(2,1)} %get-tuple-element.123, bf16[2048,128]{1,0:T(8,128)(2,1)S(1)} %get-tuple-element.75), kind=kOutput, calls=%fused_computation.21 | convolution fusion | flops 536870912 | bytes 5242880 | tf_op jit(solution)/shard_map/cond/branch_1_fun/bkc,kr->bcr/dot_general | solution.py:45
  141.8 6.6 %all-to-all-done.5 = bf16[4,256,128]{2,1,0:T(8,128)(2,1)S(1)} async-done(((bf16[4,256,128]{2,1,0:T(8,128)(2,1)}), bf16[4,256,128]{2,1,0:T(8,128)(2,1)S(1)}, u32[]{:S(2)}, u32[]{:S(2)}) %all-to-all-start.5) | async-done | bytes 262176 | tf_op jit(solution)/shard_map/all_to_all | solution.py:88
  148.5 4.9 %conditional.11 = (bf16[1024,128]{1,0:T(8,128)(2,1)S(1)}) conditional(s32[]{:T(128)} %convert_element_type.30, () %tuple.41, (bf16[8,1024,128]{2,1,0:T(8,128)(2,1)S(1)}, bf16[4,256,128]{2,1,0:T(8,128)(2,1)S(1)}, f32[1,1024]{1,0:T(1,128)S(1)}) %tuple.92), branch_computations={%region_12.13_spmd, %region_13.14_spmd} | conditional | flops 268828672 | bytes 6819848 | solution.py:90
  153.5 6.4 %collective-permute-done.7 = bf16[1024,128]{1,0:T(8,128)(2,1)S(1)} collective-permute-done((bf16[1024,128]{1,0:T(8,128)(2,1)S(1)}, bf16[1024,128]{1,0:T(8,128)(2,1)S(1)}, u32[]{:S(2)}, u32[]{:S(2)}) %collective-permute-start.7) | collective-permute-done | bytes 262176 | tf_op jit(solution)/shard_map/ppermute | solution.py:12
  159.8 6.4 %collective-permute-done.8 = bf16[1024,128]{1,0:T(8,128)(2,1)S(1)} collective-permute-done((bf16[1024,128]{1,0:T(8,128)(2,1)S(1)}, bf16[1024,128]{1,0:T(8,128)(2,1)S(1)}, u32[]{:S(2)}, u32[]{:S(2)}) %collective-permute-start.8) | collective-permute-done | bytes 262176 | tf_op jit(solution)/shard_map/ppermute | solution.py:12
  (69 shorter events, 31.4 us)
Async XLA Ops:
  6.5 0.9 copy-start
  6.5 22.0 %all-gather.5.cloned.1.call-start = ((), (), s32[]{:S(2)}) async-start(), calls=%async_computation.7 | async-start | bytes 6291456 | tf_op jit(solution)/shard_map/all_gather | solution.py:63
  6.5 7.3 %copy-start.2 = (s32[1,8,16]{2,1,0:T(8,128)S(1)}, s32[1,8,16]{2,1,0:T(8,128)}, u32[]{:S(2)}) copy-start(s32[1,8,16]{2,1,0:T(8,128)} %param.24) | copy-start | bytes 1540
  6.5 8.2 %copy-start.3 = (s32[1,8,8]{2,1,0:T(8,128)S(1)}, s32[1,8,8]{2,1,0:T(8,128)}, u32[]{:S(2)}) copy-start(s32[1,8,8]{2,1,0:T(8,128)} %param.25) | copy-start | bytes 772
  8.2 13.8 %all-to-all-start = ((bf16[4,256,128]{2,1,0:T(8,128)(2,1)}), bf16[4,256,128]{2,1,0:T(8,128)(2,1)S(1)}, u32[]{:S(2)}, u32[]{:S(2)}) async-start(bf16[4,256,128]{2,1,0:T(8,128)(2,1)} %bitcast.34), calls=%async_computation | async-start | bytes 524288 | tf_op jit(solution)/shard_map/all_to_all | solution.py:78
  13.1 33.2 %all-gather.3.cloned.1.call-start = ((), (), s32[]{:S(2)}) async-start(), calls=%async_computation.6 | async-start | bytes 3145728 | tf_op jit(solution)/shard_map/all_gather | solution.py:64
  13.1 43.1 %collective-permute-start = (bf16[1024,128]{1,0:T(8,128)(2,1)S(1)}, bf16[1024,128]{1,0:T(8,128)(2,1)S(1)}, u32[]{:S(2)}, u32[]{:S(2)}) collective-permute-start(bf16[1024,128]{1,0:T(8,128)(2,1)S(1)} %bitcast.108), channel_id=1, source_target_pairs={{0,2},{2,0},{1,3},{3,1},{4,6},{6,4},{5,7},{7,5},{8,10},{10,8},{9,1... | collective-permute-start | bytes 786440 | tf_op jit(solution)/shard_map/ppermute | solution.py:12
  22.0 6.4 %collective-permute-start.1 = (bf16[1024,128]{1,0:T(8,128)(2,1)S(1)}, bf16[1024,128]{1,0:T(8,128)(2,1)S(1)}, u32[]{:S(2)}, u32[]{:S(2)}) collective-permute-start(bf16[1024,128]{1,0:T(8,128)(2,1)S(1)} %bitcast.104), channel_id=1, source_target_pairs={{0,4},{4,0},{8,12},{12,8},{1,5},{5,1},{9,13},{13,9},{2,6},{6,2},{1... | collective-permute-start | bytes 786440 | tf_op jit(solution)/shard_map/ppermute | solution.py:22
  33.9 7.8 %copy-start.1 = (f32[1,1024]{1,0:T(1,128)S(1)}, f32[1,1024]{1,0:T(1,128)}, u32[]{:S(2)}) copy-start(f32[1,1024]{1,0:T(1,128)} %param.22) | copy-start | bytes 12292
  42.4 12.4 %all-to-all-start.1 = ((bf16[4,256,128]{2,1,0:T(8,128)(2,1)}), bf16[4,256,128]{2,1,0:T(8,128)(2,1)S(1)}, u32[]{:S(2)}, u32[]{:S(2)}) async-start(bf16[4,256,128]{2,1,0:T(8,128)(2,1)} %bitcast.36), calls=%async_computation.1 | async-start | bytes 524288 | tf_op jit(solution)/shard_map/all_to_all | solution.py:88
  50.0 4.8 %copy-start.4 = (f32[1,1024]{1,0:T(1,128)S(1)}, f32[1,1024]{1,0:T(1,128)}, u32[]{:S(2)}) copy-start(f32[1,1024]{1,0:T(1,128)} %param.23) | copy-start | bytes 12292
  54.9 14.7 %collective-permute-start.2 = (bf16[1024,128]{1,0:T(8,128)(2,1)S(1)}, bf16[1024,128]{1,0:T(8,128)(2,1)S(1)}, u32[]{:S(2)}, u32[]{:S(2)}) collective-permute-start(bf16[1024,128]{1,0:T(8,128)(2,1)S(1)} %get-tuple-element.136), channel_id=1, source_target_pairs={{0,2},{1,3},{4,6},{5,7},{8,10},{9,11},{12,14},{13,15},{16,18},{17,... | collective-permute-start | bytes 786440 | tf_op jit(solution)/shard_map/ppermute | solution.py:28
  82.9 6.4 %collective-permute-start.3 = (bf16[1024,128]{1,0:T(8,128)(2,1)S(1)}, bf16[1024,128]{1,0:T(8,128)(2,1)S(1)}, u32[]{:S(2)}, u32[]{:S(2)}) collective-permute-start(bf16[1024,128]{1,0:T(8,128)(2,1)S(1)} %bitcast.106), channel_id=1, source_target_pairs={{0,4},{4,0},{8,12},{12,8},{1,5},{5,1},{9,13},{13,9},{2,6},{6,2},{1... | collective-permute-start | bytes 786440 | tf_op jit(solution)/shard_map/ppermute | solution.py:22
  93.7 10.2 %all-to-all-start.3 = ((bf16[4,256,128]{2,1,0:T(8,128)(2,1)}), bf16[4,256,128]{2,1,0:T(8,128)(2,1)S(1)}, u32[]{:S(2)}, u32[]{:S(2)}) async-start(bf16[4,256,128]{2,1,0:T(8,128)(2,1)} %bitcast.39), calls=%async_computation.3 | async-start | bytes 524288 | tf_op jit(solution)/shard_map/all_to_all | solution.py:88
  108.8 8.3 %collective-permute-start.4 = (bf16[1024,128]{1,0:T(8,128)(2,1)S(1)}, bf16[1024,128]{1,0:T(8,128)(2,1)S(1)}, u32[]{:S(2)}, u32[]{:S(2)}) collective-permute-start(bf16[1024,128]{1,0:T(8,128)(2,1)S(1)} %get-tuple-element.138), channel_id=1, source_target_pairs={{0,2},{1,3},{4,6},{5,7},{8,10},{9,11},{12,14},{13,15},{16,18},{17,... | collective-permute-start | bytes 786440 | tf_op jit(solution)/shard_map/ppermute | solution.py:28
  127.4 6.4 %collective-permute-start.5 = (bf16[1024,128]{1,0:T(8,128)(2,1)S(1)}, bf16[1024,128]{1,0:T(8,128)(2,1)S(1)}, u32[]{:S(2)}, u32[]{:S(2)}) collective-permute-start(bf16[1024,128]{1,0:T(8,128)(2,1)S(1)} %bitcast.105), channel_id=1, source_target_pairs={{0,4},{4,0},{8,12},{12,8},{1,5},{5,1},{9,13},{13,9},{2,6},{6,2},{1... | collective-permute-start | bytes 786440 | tf_op jit(solution)/shard_map/ppermute | solution.py:22
  138.3 10.2 %all-to-all-start.5 = ((bf16[4,256,128]{2,1,0:T(8,128)(2,1)}), bf16[4,256,128]{2,1,0:T(8,128)(2,1)S(1)}, u32[]{:S(2)}, u32[]{:S(2)}) async-start(bf16[4,256,128]{2,1,0:T(8,128)(2,1)} %bitcast.42), calls=%async_computation.5 | async-start | bytes 524288 | tf_op jit(solution)/shard_map/all_to_all | solution.py:88
  141.8 11.6 %collective-permute-start.6 = (bf16[1024,128]{1,0:T(8,128)(2,1)S(1)}, bf16[1024,128]{1,0:T(8,128)(2,1)S(1)}, u32[]{:S(2)}, u32[]{:S(2)}) collective-permute-start(bf16[1024,128]{1,0:T(8,128)(2,1)S(1)} %broadcast_select_fusion.9), channel_id=1, source_target_pairs={{0,2},{2,0},{1,3},{3,1},{4,6},{6,4},{5,7},{7,5},{8,10},{10,8},{9,1... | collective-permute-start | bytes 786440 | tf_op jit(solution)/shard_map/ppermute | solution.py:12
  153.4 6.4 %collective-permute-start.7 = (bf16[1024,128]{1,0:T(8,128)(2,1)S(1)}, bf16[1024,128]{1,0:T(8,128)(2,1)S(1)}, u32[]{:S(2)}, u32[]{:S(2)}) collective-permute-start(bf16[1024,128]{1,0:T(8,128)(2,1)S(1)} %broadcast_select_fusion.8), channel_id=1, source_target_pairs={{0,2},{2,0},{1,3},{3,1},{4,6},{6,4},{5,7},{7,5},{8,10},{10,8},{9,1... | collective-permute-start | bytes 786440 | tf_op jit(solution)/shard_map/ppermute | solution.py:12
  159.8 6.4 %collective-permute-start.8 = (bf16[1024,128]{1,0:T(8,128)(2,1)S(1)}, bf16[1024,128]{1,0:T(8,128)(2,1)S(1)}, u32[]{:S(2)}, u32[]{:S(2)}) collective-permute-start(bf16[1024,128]{1,0:T(8,128)(2,1)S(1)} %collective-permute-done.7), channel_id=1, source_target_pairs={{0,2},{2,0},{1,3},{3,1},{4,6},{6,4},{5,7},{7,5},{8,10},{10,8},{9,1... | collective-permute-start | bytes 786440 | tf_op jit(solution)/shard_map/ppermute | solution.py:12
Sparse Core Ops, SparseCore 0:
  8.9 15.1 all-gather.4
  25.6 11.7 all-gather.2
where the time goes:
time: 176 us; the launch traced here: 174 us
  waiting for transfers between devices  69.5 us (39%)
  blocking collectives  23.6 us (13%)
  starting transfers between devices  21.9 us (12%)
  other arithmetic  16.9 us (10%)
  local copies, waits for them, and re-layouts  16.6 us (9%)
  between operations  13.6 us (8%)
  matrix products  11.5 us (7%)
    all_to_all x2, blocking collectives, body(): lax.all_to_all(incoming, 'owners', split_axis=0, concat_axis=0, tiled=True)  23.6 us
    ppermute x2, waiting for transfers between devices, passed_along(): return lax.ppermute(array, axis, pairs)  20.3 us
    ppermute x3, waiting for transfers between devices, swapped(): return lax.ppermute(block, axis, route)  15.7 us
    all_to_all x3, waiting for transfers between devices, body(): lax.all_to_all(middle, 'owners', split_axis=0, concat_axis=0, tiled=True)  13.4 us
    ppermute x4, waiting for transfers between devices, from_behind(): return lax.ppermute(value, axis, pairs)  12.7 us
    select_n x2, other arithmetic, order_tiles(): ordered = jnp.take_along_axis(shaped, inverse[:, :, None, None], axis=1)  12.6 us
    dot_general x4, matrix products, mixed_layer(): jnp.einsum('bkc,kr->bcr', ordered, group_rows, preferred_element_type=jnp...  11.5 us
    all_to_all x3, starting transfers between devices, body(): lax.all_to_all(middle, 'owners', split_axis=0, concat_axis=0, tiled=True)  10.6 us
  transfers between devices with their start and end apart: 15, of which 10 were waited for; matrix products, arithmetic and copies ran while one was open for 17% of the time, Pallas kernels for 0%

commit v1 on v0

v1 whole, which is shorter than its diff:
```python
import functools
import math

import jax
import jax.numpy as jnp
from jax import lax
from jax.experimental import pallas as pl
from jax.experimental.pallas import tpu as pltpu
from jax.sharding import PartitionSpec as P

CEILING = 4.0
MESH = pl.DeviceIdType.MESH


def relay(dims, x, w1, w2, b1, b2, l1, l2, o, raw1, far1, raw2, far2, til1, til2, col1, col2,
          in_a, in_b, mid, res, acc, s_w, r_w, l_w, s_in, s_a, r_a, s_b, r_b, s_o, r_o):
    n, sections, span, chunks, tile = dims
    me = lax.axis_index("owners")
    sec = lax.axis_index("section")
    rep = lax.axis_index("rep")
    piece = x.shape[1]
    width = n * piece
    rows = x.shape[2]
    blocks = width // tile
    half = w1.shape[0]
    per = n // chunks
    sub = blocks // chunks
    last = sections - 1

    barrier = pltpu.get_barrier_semaphore()
    for t in range(sections):
        for w in range(n):
            @pl.when(jnp.logical_or(me != w, sec != t))
            def _():
                pl.semaphore_signal(barrier, inc=1, device_id={"owners": w, "section": t}, device_id_type=MESH)
    pl.semaphore_signal(barrier, inc=1, device_id={"rep": 1 - rep}, device_id_type=MESH)

    local = [
        pltpu.make_async_copy(w1, raw1, l_w.at[0]),
        pltpu.make_async_copy(w2, raw2, l_w.at[1]),
    ]
    for copy in local:
        copy.start()
    pl.semaphore_wait(barrier, n * sections)

    def pair_of(w):
        return (w // span) * span

    def send_a(src, m_slot, w, target, send_sem, recv_sem):
        return pltpu.make_async_remote_copy(
            src_ref=src.at[pl.ds(pair_of(w), span)],
            dst_ref=in_a.at[m_slot, :, me],
            send_sem=send_sem, recv_sem=recv_sem,
            device_id={"owners": w, "section": target}, device_id_type=MESH)

    def own_in():
        return pltpu.make_async_copy(x.at[pl.ds(pair_of(me), span)], in_a.at[0, :, me], r_a.at[0, me])

    for d in range(n - 1, -1, -1):
        w = lax.rem(me + d, n)
        if d == 0:
            @pl.when(sec == 0)
            def _():
                own_in().start()

            @pl.when(sec != 0)
            def _():
                send_a(x, sec, w, 0, s_in.at[d], r_a.at[sec, me]).start()
        else:
            send_a(x, sec, w, 0, s_in.at[d], r_a.at[sec, me]).start()

    def weight_copy(src, dst, k):
        return pltpu.make_async_remote_copy(
            src_ref=src, dst_ref=dst,
            send_sem=s_w.at[k], recv_sem=r_w.at[k],
            device_id={"rep": 1 - rep}, device_id_type=MESH)

    weight_copy(w1, far1, 0).start()
    weight_copy(w2, far2, 1).start()

    def arrange(raw, til, links, begin, spans):
        radix = spans * blocks

        def one(b, carry):
            i = b + begin
            taken = [links[i, k] for k in range(radix)]
            for p in range(radix):
                slot = jnp.int32(0)
                for k in range(1, radix):
                    slot = jnp.where(taken[k] == p, k, slot)
                h, j = p // blocks, p % blocks
                c, q = j // sub, h * sub + j % sub
                til[c, pl.ds(pl.multiple_of(i * tile, tile), tile), q * tile:(q + 1) * tile] = raw[b, slot].T
            return carry

        lax.fori_loop(0, half, one, 0)

    def bias_columns(b, col):
        for i in range(blocks):
            row = b[0:1, i * tile:(i + 1) * tile]
            col[i * tile:(i + 1) * tile, :] = jnp.broadcast_to(row, (rows, tile)).T

    bias_columns(b1, col1)
    bias_columns(b2, col2)
    local[0].wait()
    arrange(raw1, til1, l1, rep * half, span)
    weight_copy(w1, far1, 0).wait_recv()
    arrange(far1, til1, l1, (1 - rep) * half, span)

    def finish(col):
        return jnp.clip(acc[...] + col[...], 0.0, CEILING).astype(jnp.bfloat16)

    mine = me // per
    for m in range(sections):
        for d in range(chunks):
            c = lax.rem(mine + d, chunks)
            for k in range(per):
                u = c * per + k
                pltpu.make_async_copy(in_a.at[m, :, u], in_a.at[m, :, u], r_a.at[m, u]).wait()
            v = in_a[m, :, pl.ds(c * per, per)].reshape(span * per * piece, rows)
            part = jnp.dot(til1[c], v, preferred_element_type=jnp.float32)
            acc[...] = part if d == 0 else acc[...] + part
        mid[m] = finish(col1).reshape(n, piece, rows)
        for d in range(n - 1, 0, -1):
            w = lax.rem(me + d, n)
            pltpu.make_async_remote_copy(
                src_ref=mid.at[m, w], dst_ref=in_b.at[m, me],
                send_sem=s_b.at[m, d], recv_sem=r_b.at[m, me],
                device_id={"owners": w}, device_id_type=MESH).start()
        in_b[m, me] = mid[m, me]
        if m == 0:
            local[1].wait()
            arrange(raw2, til2, l2, rep * half, 1)
            weight_copy(w2, far2, 1).wait_recv()
            arrange(far2, til2, l2, (1 - rep) * half, 1)
        for d in range(chunks):
            c = lax.rem(mine + d, chunks)
            for k in range(per):
                u = c * per + k
                if d == 0:
                    @pl.when(u != me)
                    def _():
                        pltpu.make_async_copy(in_b.at[m, u], in_b.at[m, u], r_b.at[m, u]).wait()
                else:
                    pltpu.make_async_copy(in_b.at[m, u], in_b.at[m, u], r_b.at[m, u]).wait()
            v = in_b[m, pl.ds(c * per, per)].reshape(per * piece, rows)
            part = jnp.dot(til2[c], v, preferred_element_type=jnp.float32)
            acc[...] = part if d == 0 else acc[...] + part
        res[m] = finish(col2).reshape(n, piece, rows)

        if last > 0:
            @pl.when(sec < last)
            def _():
                for d in range(n - 1, -1, -1):
                    send_a(res.at[m], m, lax.rem(me + d, n), sec + 1, s_a.at[m, d], r_a.at[m, me]).start()

        @pl.when(sec == last)
        def _():
            if m == last:
                o[...] = res[m]
            else:
                pltpu.make_async_remote_copy(
                    src_ref=res.at[m], dst_ref=o, send_sem=s_o.at[m], recv_sem=r_o.at[0],
                    device_id={"section": m}, device_id_type=MESH).start()

    def sent(ref, sem):
        pltpu.make_async_copy(ref, ref, sem).wait()

    for d in range(n):
        if d == 0:
            @pl.when(sec != 0)
            def _():
                sent(in_a.at[0, :, 0], s_in.at[d])
        else:
            sent(in_a.at[0, :, 0], s_in.at[d])
    for m in range(sections):
        for d in range(1, n):
            sent(mid.at[m, 0], s_b.at[m, d])
    weight_copy(w1, far1, 0).wait_send()
    weight_copy(w2, far2, 1).wait_send()
    if last > 0:
        @pl.when(sec < last)
        def _():
            for m in range(sections):
                for d in range(n):
                    sent(in_a.at[m, :, 0], s_a.at[m, d])
            sent(o, r_o.at[0])

        @pl.when(sec == last)
        def _():
            for m in range(last):
                sent(res.at[m], s_o.at[m])


def body(inputs, weight_first, weight_second, bias_first, bias_second, links_first, links_second):
    n = lax.axis_size("owners")
    sections = lax.axis_size("section")
    width, rows = inputs.shape[1:]
    half, deep, tile = weight_first.shape[1:]
    radix_a = links_first.shape[2]
    radix_b = links_second.shape[2]
    blocks = width // tile
    span = radix_a // blocks
    piece = width // n
    chunks = math.gcd(math.gcd(n, blocks), 4)
    dims = (n, sections, span, chunks, tile)
    bf = jnp.bfloat16
    anyspace = pl.BlockSpec(memory_space=pl.ANY)
    vmem = pl.BlockSpec(memory_space=pltpu.VMEM)
    smem = pl.BlockSpec(memory_space=pltpu.SMEM)
    dma = pltpu.SemaphoreType.DMA
    out = pl.pallas_call(
        functools.partial(relay, dims),
        name="relay",
        out_shape=jax.ShapeDtypeStruct((n, piece, rows), bf),
        in_specs=[anyspace, anyspace, anyspace, vmem, vmem, smem, smem],
        out_specs=vmem,
        scratch_shapes=[
            pltpu.VMEM((half, radix_a, tile, tile), bf),
            pltpu.VMEM((half, radix_a, tile, tile), bf),
            pltpu.VMEM((half, radix_b, tile, tile), bf),
            pltpu.VMEM((half, radix_b, tile, tile), bf),
            pltpu.VMEM((chunks, width, radix_a * tile // chunks), bf),
            pltpu.VMEM((chunks, width, radix_b * tile // chunks), bf),
            pltpu.VMEM((width, rows), jnp.float32),
            pltpu.VMEM((width, rows), jnp.float32),
            pltpu.VMEM((sections, span, n, piece, rows), bf),
            pltpu.VMEM((sections, n, piece, rows), bf),
            pltpu.VMEM((sections, n, piece, rows), bf),
            pltpu.VMEM((sections, n, piece, rows), bf),
            pltpu.VMEM((width, rows), jnp.float32),
            dma((2,)), dma((2,)), dma((2,)),
            dma((n,)), dma((sections, n)), dma((sections, n)),
            dma((sections, n)), dma((sections, n)),
            dma((sections,)), dma((1,)),
        ],
        compiler_params=pltpu.CompilerParams(
            collective_id=0, has_side_effects=True, vmem_limit_bytes=40 * 1024 * 1024),
    )(
        inputs.reshape(n, piece, rows),
        weight_first.reshape(half, radix_a, tile, tile),
        weight_second.reshape(half, radix_b, tile, tile),
        bias_first, bias_second, links_first[0], links_second[0],
    )
    return out.reshape(1, width, rows)


def solution(mesh):
    placed = (
        P("section", "owners", ("groups", "rep")),
        P("section", ("owners", "rep"), None, None),
        P("section", ("owners", "rep"), None, None),
        P("section", "owners"),
        P("section", "owners"),
        P("section", "owners", None),
        P("section", "owners", None),
    )
    return jax.shard_map(
        body,
        mesh=mesh,
        in_specs=placed,
        out_specs=P("section", "owners", ("groups", "rep")),
        check_vma=False,
    )
```

time: 176 us -> 67.8 us (0.39); the launches traced: 174 us -> 67.5 us
  waiting for transfers between devices: 69.5 us -> 0 us
  Pallas kernels: 0 us -> 60.2 us
  blocking collectives: 23.6 us -> 0 us
  starting transfers between devices: 21.9 us -> 0 us
  other arithmetic: 16.9 us -> 0 us
  between operations: 13.6 us -> 0.02 us
  matrix products: 11.5 us -> 0 us
  local copies, waits for them, and re-layouts: 16.6 us -> 7.21 us
    pallas_call x0 -> x1, Pallas kernels: none -> 60.2 us  [body(): pl.pallas_call(functools.partial(relay, dims), name='relay', out_shape=ja...]
    ppermute x9 -> x0, waiting for transfers between devices: 48.8 us -> none  [the longest x2 20.3 us: passed_along(): return lax.ppermute(array, axis, pairs)]
    all_to_all x2 -> x0, blocking collectives: 23.6 us -> none  [body(): lax.all_to_all(incoming, 'owners', split_axis=0, concat_axis=0, tiled=True)]
    all_to_all x4 -> x0, waiting for transfers between devices: 19.8 us -> none  [the longest x3 13.4 us: body(): lax.all_to_all(middle, 'owners', split_axis=0, concat_axis=0, tiled=True)]
    all_to_all x4 -> x0, starting transfers between devices: 15.4 us -> none  [the longest x3 10.6 us: body(): lax.all_to_all(middle, 'owners', split_axis=0, concat_axis=0, tiled=True)]
    select_n x9 -> x0, other arithmetic: 13.5 us -> none  [the longest x2 12.6 us: order_tiles(): ordered = jnp.take_along_axis(shaped, inverse[:, :, None, None], axis=1)]
    dot_general x4 -> x0, matrix products: 11.5 us -> none  [mixed_layer(): jnp.einsum('bkc,kr->bcr', ordered, group_rows, preferred_element_type=jnp...]
    gather x6 -> x0, local copies, waits for them, and re-layouts: 9.4 us -> none  [order_tiles(): ordered = jnp.take_along_axis(shaped, inverse[:, :, None, None], axis=1)]
  transfers between devices with their start and end apart: 15 -> 0, of which waited for: 10 -> 0; matrix products, arithmetic and copies ran while one was open for 17% -> 0% of each run, Pallas kernels for 0% -> 0%
where the time goes in v1:
time: 67.8 us; the launch traced here: 67.5 us
  Pallas kernels  60.2 us (89%)
  local copies, waits for them, and re-layouts  7.21 us (11%)
    pallas_call x1, Pallas kernels, body(): pl.pallas_call(functools.partial(relay, dims), name='relay', out_shape=ja...  60.2 us
    unnamed x15, local copies, waits for them, and re-layouts  7.21 us

profile of v1, /device:TPU:6, one launch (start us, length us, event | category | flops | bytes accessed | tf_op | source)
XLA Modules:
  0.0 67.5 jit_solution(18158897403474879109)
XLA Ops:
  0.0 0.0 copy-start
  0.0 1.6 %copy-done = bf16[1,4,2048,128]{3,2,1,0:T(8,128)(2,1)S(1)} copy-done((bf16[1,4,2048,128]{3,2,1,0:T(8,128)(2,1)S(1)}, bf16[1,4,2048,128]{3,2,1,0:T(8,128)(2,1)}, u32[]{:S(2)}) %copy-start) | copy-done | bytes 2097176
  1.6 0.0 copy-start.1
  1.6 1.2 %copy-done.1 = bf16[1,4,1024,128]{3,2,1,0:T(8,128)(2,1)S(1)} copy-done((bf16[1,4,1024,128]{3,2,1,0:T(8,128)(2,1)S(1)}, bf16[1,4,1024,128]{3,2,1,0:T(8,128)(2,1)}, u32[]{:S(2)}) %copy-start.1) | copy-done | bytes 1048600
  2.8 0.0 copy-start.2
  2.8 0.9 %copy-done.2 = bf16[1,1024,128]{2,1,0:T(8,128)(2,1)S(1)} copy-done((bf16[1,1024,128]{2,1,0:T(8,128)(2,1)S(1)}, bf16[1,1024,128]{2,1,0:T(8,128)(2,1)}, u32[]{:S(2)}) %copy-start.2) | copy-done | bytes 262168
  3.8 0.0 copy-start.3
  3.8 0.7 %copy-done.3 = f32[1,1024]{1,0:T(1,128)S(1)} copy-done((f32[1,1024]{1,0:T(1,128)S(1)}, f32[1,1024]{1,0:T(1,128)}, u32[]{:S(2)}) %copy-start.3) | copy-done | bytes 4120
  4.5 0.0 copy-start.4
  4.5 0.7 %copy-done.4 = f32[1,1024]{1,0:T(1,128)S(1)} copy-done((f32[1,1024]{1,0:T(1,128)S(1)}, f32[1,1024]{1,0:T(1,128)}, u32[]{:S(2)}) %copy-start.4) | copy-done | bytes 4120
  5.1 0.0 copy-start.5
  5.1 0.7 %copy-done.5 = s32[1,8,16]{2,1,0:T(8,128)S(1)} copy-done((s32[1,8,16]{2,1,0:T(8,128)S(1)}, s32[1,8,16]{2,1,0:T(8,128)}, u32[]{:S(2)}) %copy-start.5) | copy-done | bytes 536
  5.8 0.0 copy-start.6
  5.8 0.7 %copy-done.6 = s32[1,8,8]{2,1,0:T(8,128)S(1)} copy-done((s32[1,8,8]{2,1,0:T(8,128)S(1)}, s32[1,8,8]{2,1,0:T(8,128)}, u32[]{:S(2)}) %copy-start.6) | copy-done | bytes 280
  6.5 60.2 %relay.1 = bf16[4,256,128]{2,1,0:T(8,128)(2,1)S(1)} custom-call(bf16[4,256,128]{2,1,0:T(8,128)(2,1)S(1)} %bitcast.9, bf16[4,16,128,128]{3,2,1,0:T(8,128)(2,1)S(1)} %bitcast.6, bf16[4,8,128,128]{3,2,1,0:T(8,128)(2,1)S(1)} %bitcast.8, f32[1,1024]{1,0:T(1,128)S(1)} %copy-done.3, f32[1,1024]{1,0:T(1,128)S(1)} %copy-done.4, s32[8,16]{1,0:T(8,128)S(1)} %bitcast.10, ...), custom_call_target="tpu_custom_call" | custom-call | tf_op jit(solution)/shard_map/relay/pallas_call | solution.py:212
  66.8 0.7 %copy.9 = bf16[1,1024,128]{2,1,0:T(8,128)(2,1)} copy(bf16[1,1024,128]{2,1,0:T(8,128)(2,1)S(1)} %bitcast.7) | data formatting | bytes 524288
Async XLA Ops:
  0.0 1.6 %copy-start = (bf16[1,4,2048,128]{3,2,1,0:T(8,128)(2,1)S(1)}, bf16[1,4,2048,128]{3,2,1,0:T(8,128)(2,1)}, u32[]{:S(2)}) copy-start(bf16[1,4,2048,128]{3,2,1,0:T(8,128)(2,1)} %param.8) | copy-start | bytes 6291460
  1.6 1.2 %copy-start.1 = (bf16[1,4,1024,128]{3,2,1,0:T(8,128)(2,1)S(1)}, bf16[1,4,1024,128]{3,2,1,0:T(8,128)(2,1)}, u32[]{:S(2)}) copy-start(bf16[1,4,1024,128]{3,2,1,0:T(8,128)(2,1)} %param.9) | copy-start | bytes 3145732
  2.8 0.9 %copy-start.2 = (bf16[1,1024,128]{2,1,0:T(8,128)(2,1)S(1)}, bf16[1,1024,128]{2,1,0:T(8,128)(2,1)}, u32[]{:S(2)}) copy-start(bf16[1,1024,128]{2,1,0:T(8,128)(2,1)} %param.7) | copy-start | bytes 786436
  3.8 0.7 %copy-start.3 = (f32[1,1024]{1,0:T(1,128)S(1)}, f32[1,1024]{1,0:T(1,128)}, u32[]{:S(2)}) copy-start(f32[1,1024]{1,0:T(1,128)} %b1.1) | copy-start | bytes 12292
  4.5 0.7 %copy-start.4 = (f32[1,1024]{1,0:T(1,128)S(1)}, f32[1,1024]{1,0:T(1,128)}, u32[]{:S(2)}) copy-start(f32[1,1024]{1,0:T(1,128)} %b2.1) | copy-start | bytes 12292
  5.1 0.7 %copy-start.5 = (s32[1,8,16]{2,1,0:T(8,128)S(1)}, s32[1,8,16]{2,1,0:T(8,128)}, u32[]{:S(2)}) copy-start(s32[1,8,16]{2,1,0:T(8,128)} %param.12) | copy-start | bytes 1540
  5.8 0.7 %copy-start.6 = (s32[1,8,8]{2,1,0:T(8,128)S(1)}, s32[1,8,8]{2,1,0:T(8,128)}, u32[]{:S(2)}) copy-start(s32[1,8,8]{2,1,0:T(8,128)} %param.13) | copy-start | bytes 772

commit v2 on v1

--- a/solution.py
+++ b/solution.py
@@ -12,8 +12,8 @@
 MESH = pl.DeviceIdType.MESH
 
 
-def relay(dims, x, w1, w2, b1, b2, l1, l2, o, raw1, far1, raw2, far2, til1, til2, col1, col2,
-          in_a, in_b, mid, res, acc, s_w, r_w, l_w, s_in, s_a, r_a, s_b, r_b, s_o, r_o):
+def relay(dims, x, w1, w2, b1_in, b2_in, l1_in, l2_in, o, b1, b2, l1, l2, raw1, far1, raw2, far2, til1, til2, col1, col2,
+          in_a, in_b, mid, res, acc, s_w, r_w, l_w, s_in, s_a, r_a, s_f, s_b, r_b, s_o, r_o):
     n, sections, span, chunks, tile = dims
     me = lax.axis_index("owners")
     sec = lax.axis_index("section")
@@ -38,36 +38,51 @@
     local = [
         pltpu.make_async_copy(w1, raw1, l_w.at[0]),
         pltpu.make_async_copy(w2, raw2, l_w.at[1]),
+        pltpu.make_async_copy(l1_in, l1, l_w.at[2]),
+        pltpu.make_async_copy(l2_in, l2, l_w.at[3]),
+        pltpu.make_async_copy(b1_in, b1, l_w.at[4]),
+        pltpu.make_async_copy(b2_in, b2, l_w.at[5]),
     ]
     for copy in local:
         copy.start()
     pl.semaphore_wait(barrier, n * sections)
 
-    def pair_of(w):
-        return (w // span) * span
-
-    def send_a(src, m_slot, w, target, send_sem, recv_sem):
-        return pltpu.make_async_remote_copy(
-            src_ref=src.at[pl.ds(pair_of(w), span)],
-            dst_ref=in_a.at[m_slot, :, me],
-            send_sem=send_sem, recv_sem=recv_sem,
-            device_id={"owners": w, "section": target}, device_id_type=MESH)
-
-    def own_in():
-        return pltpu.make_async_copy(x.at[pl.ds(pair_of(me), span)], in_a.at[0, :, me], r_a.at[0, me])
-
-    for d in range(n - 1, -1, -1):
-        w = lax.rem(me + d, n)
-        if d == 0:
-            @pl.when(sec == 0)
-            def _():
-                own_in().start()
-
-            @pl.when(sec != 0)
-            def _():
-                send_a(x, sec, w, 0, s_in.at[d], r_a.at[sec, me]).start()
-        else:
-            send_a(x, sec, w, 0, s_in.at[d], r_a.at[sec, me]).start()
+    par = lax.rem(me, span)
+    base = me - par
+    classes = n // span
+    bytes_of = in_a.at[0, 0, 0]
+
+    def fellow(k):
+        return lax.rem(me + span * k, n)
+
+    def mate(j):
+        return base + lax.rem(par + j, span)
+
+    def send_a(src, slot, h, w, target, sem):
+        pltpu.make_async_remote_copy(
+            src_ref=src.at[(w // span) * span + h], dst_ref=in_a.at[slot, h, me],
+            send_sem=sem.at[h, w], recv_sem=r_a.at[slot, h, me],
+            device_id={"owners": w, "section": target}, device_id_type=MESH).start()
+
+    def done(sem):
+        pltpu.make_async_copy(bytes_of, bytes_of, sem).wait()
+
+    def home_targets():
+        return [fellow(k) for k in range(1, classes)] + [mate(j) for j in range(1, span)]
+
+    @pl.when(sec == 0)
+    def _():
+        for w in home_targets():
+            for h in range(span):
+                send_a(x, 0, h, w, 0, s_in)
+        for h in range(span):
+            pltpu.make_async_copy(x.at[base + h], in_a.at[0, h, me], r_a.at[0, h, me]).start()
+
+    @pl.when(sec != 0)
+    def _():
+        for d in range(n - 1, -1, -1):
+            for h in range(span):
+                send_a(x, sec + 1, h, lax.rem(me + d, n), 0, s_in)
 
     def weight_copy(src, dst, k):
         return pltpu.make_async_remote_copy(
@@ -100,6 +115,8 @@
             row = b[0:1, i * tile:(i + 1) * tile]
             col[i * tile:(i + 1) * tile, :] = jnp.broadcast_to(row, (rows, tile)).T
 
+    for copy in local[2:]:
+        copy.wait()
     bias_columns(b1, col1)
     bias_columns(b2, col2)
     local[0].wait()
@@ -111,15 +128,55 @@
         return jnp.clip(acc[...] + col[...], 0.0, CEILING).astype(jnp.bfloat16)
 
     mine = me // per
-    for m in range(sections):
-        for d in range(chunks):
+    order = sorted(range(chunks), key=lambda d: (d % span, d))
+
+    def slot_of(m):
+        return jnp.where(sec == 0, 0, 1) if m == 0 else m + 1
+
+    def forward(m, h, u, j):
+        slot = slot_of(m)
+        return pltpu.make_async_remote_copy(
+            src_ref=in_a.at[slot, h, u], dst_ref=in_a.at[slot, h, u],
+            send_sem=s_f.at[m, h, u, j - 1], recv_sem=r_a.at[slot, h, u],
+            device_id={"owners": mate(j)}, device_id_type=MESH)
+
+    def forwards(m, act):
+        for k in range(classes):
+            def go():
+                for h in range(span):
+                    for j in range(1, span):
+                        act(forward(m, h, fellow(k), j))
+            if m == 0 and k > 0:
+                go()
+            else:
+                pl.when(sec > 0)(go)
+
+    def first_layer(m):
+        slot = slot_of(m)
+        for k in range(classes):
+            u = fellow(k)
+            for h in range(span):
+                done(r_a.at[slot, h, u])
+
+                def go():
+                    for j in range(1, span):
+                        forward(m, h, u, j).start()
+                if m == 0 and k > 0:
+                    go()
+                else:
+                    pl.when(sec > 0)(go)
+        for e, d in enumerate(order):
             c = lax.rem(mine + d, chunks)
             for k in range(per):
                 u = c * per + k
-                pltpu.make_async_copy(in_a.at[m, :, u], in_a.at[m, :, u], r_a.at[m, u]).wait()
-            v = in_a[m, :, pl.ds(c * per, per)].reshape(span * per * piece, rows)
+
+                @pl.when(lax.rem(u, span) != par)
+                def _():
+                    for h in range(span):
+                        done(r_a.at[slot, h, u])
+            v = in_a[slot, :, pl.ds(c * per, per)].reshape(span * per * piece, rows)
             part = jnp.dot(til1[c], v, preferred_element_type=jnp.float32)
-            acc[...] = part if d == 0 else acc[...] + part
+            acc[...] = part if e == 0 else acc[...] + part
         mid[m] = finish(col1).reshape(n, piece, rows)
         for d in range(n - 1, 0, -1):
             w = lax.rem(me + d, n)
@@ -128,11 +185,8 @@
                 send_sem=s_b.at[m, d], recv_sem=r_b.at[m, me],
                 device_id={"owners": w}, device_id_type=MESH).start()
         in_b[m, me] = mid[m, me]
-        if m == 0:
-            local[1].wait()
-            arrange(raw2, til2, l2, rep * half, 1)
-            weight_copy(w2, far2, 1).wait_recv()
-            arrange(far2, til2, l2, (1 - rep) * half, 1)
+
+    def second_layer(m):
         for d in range(chunks):
             c = lax.rem(mine + d, chunks)
             for k in range(per):
@@ -140,9 +194,9 @@
                 if d == 0:
                     @pl.when(u != me)
                     def _():
-                        pltpu.make_async_copy(in_b.at[m, u], in_b.at[m, u], r_b.at[m, u]).wait()
+                        done(r_b.at[m, u])
                 else:
-                    pltpu.make_async_copy(in_b.at[m, u], in_b.at[m, u], r_b.at[m, u]).wait()
+                    done(r_b.at[m, u])
             v = in_b[m, pl.ds(c * per, per)].reshape(per * piece, rows)
             part = jnp.dot(til2[c], v, preferred_element_type=jnp.float32)
             acc[...] = part if d == 0 else acc[...] + part
@@ -151,8 +205,9 @@
         if last > 0:
             @pl.when(sec < last)
             def _():
-                for d in range(n - 1, -1, -1):
-                    send_a(res.at[m], m, lax.rem(me + d, n), sec + 1, s_a.at[m, d], r_a.at[m, me]).start()
+                for k in range(classes - 1, -1, -1):
+                    for h in range(span):
+                        send_a(res.at[m], m + 1, h, fellow(k), sec + 1, s_a.at[m])
 
         @pl.when(sec == last)
         def _():
@@ -163,17 +218,32 @@
                     src_ref=res.at[m], dst_ref=o, send_sem=s_o.at[m], recv_sem=r_o.at[0],
                     device_id={"section": m}, device_id_type=MESH).start()
 
+    first_layer(0)
+    local[1].wait()
+    arrange(raw2, til2, l2, rep * half, 1)
+    weight_copy(w2, far2, 1).wait_recv()
+    arrange(far2, til2, l2, (1 - rep) * half, 1)
+    for m in range(sections):
+        if m < last:
+            first_layer(m + 1)
+        second_layer(m)
+
     def sent(ref, sem):
         pltpu.make_async_copy(ref, ref, sem).wait()
 
-    for d in range(n):
-        if d == 0:
-            @pl.when(sec != 0)
-            def _():
-                sent(in_a.at[0, :, 0], s_in.at[d])
-        else:
-            sent(in_a.at[0, :, 0], s_in.at[d])
+    @pl.when(sec == 0)
+    def _():
+        for w in home_targets():
+            for h in range(span):
+                done(s_in.at[h, w])
+
+    @pl.when(sec != 0)
+    def _():
+        for w in range(n):
+            for h in range(span):
+                done(s_in.at[h, w])
     for m in range(sections):
+        forwards(m, lambda copy: copy.wait_send())
         for d in range(1, n):
             sent(mid.at[m, 0], s_b.at[m, d])
     weight_copy(w1, far1, 0).wait_send()
@@ -182,8 +252,9 @@
         @pl.when(sec < last)
         def _():
             for m in range(sections):
-                for d in range(n):
-                    sent(in_a.at[m, :, 0], s_a.at[m, d])
+                for k in range(classes):
+                    for h in range(span):
+                        done(s_a.at[m, h, fellow(k)])
             sent(o, r_o.at[0])
 
         @pl.when(sec == last)
@@ -205,17 +276,20 @@
     chunks = math.gcd(math.gcd(n, blocks), 4)
     dims = (n, sections, span, chunks, tile)
     bf = jnp.bfloat16
-    anyspace = pl.BlockSpec(memory_space=pl.ANY)
+    anyspace = pl.BlockSpec(memory_space=pltpu.HBM)
     vmem = pl.BlockSpec(memory_space=pltpu.VMEM)
-    smem = pl.BlockSpec(memory_space=pltpu.SMEM)
     dma = pltpu.SemaphoreType.DMA
     out = pl.pallas_call(
         functools.partial(relay, dims),
         name="relay",
         out_shape=jax.ShapeDtypeStruct((n, piece, rows), bf),
-        in_specs=[anyspace, anyspace, anyspace, vmem, vmem, smem, smem],
+        in_specs=[anyspace] * 7,
         out_specs=vmem,
         scratch_shapes=[
+            pltpu.VMEM(bias_first.shape, jnp.float32),
+            pltpu.VMEM(bias_second.shape, jnp.float32),
+            pltpu.SMEM(links_first.shape[1:], jnp.int32),
+            pltpu.SMEM(links_second.shape[1:], jnp.int32),
             pltpu.VMEM((half, radix_a, tile, tile), bf),
             pltpu.VMEM((half, radix_a, tile, tile), bf),
             pltpu.VMEM((half, radix_b, tile, tile), bf),
@@ -224,18 +298,19 @@
             pltpu.VMEM((chunks, width, radix_b * tile // chunks), bf),
             pltpu.VMEM((width, rows), jnp.float32),
             pltpu.VMEM((width, rows), jnp.float32),
-            pltpu.VMEM((sections, span, n, piece, rows), bf),
+            pltpu.VMEM((sections + 1, span, n, piece, rows), bf),
             pltpu.VMEM((sections, n, piece, rows), bf),
             pltpu.VMEM((sections, n, piece, rows), bf),
             pltpu.VMEM((sections, n, piece, rows), bf),
             pltpu.VMEM((width, rows), jnp.float32),
-            dma((2,)), dma((2,)), dma((2,)),
-            dma((n,)), dma((sections, n)), dma((sections, n)),
+            dma((2,)), dma((2,)), dma((6,)),
+            dma((span, n)), dma((sections, span, n)), dma((sections + 1, span, n)),
+            dma((sections, span, n, max(span - 1, 1))),
             dma((sections, n)), dma((sections, n)),
             dma((sections,)), dma((1,)),
         ],
         compiler_params=pltpu.CompilerParams(
-            collective_id=0, has_side_effects=True, vmem_limit_bytes=40 * 1024 * 1024),
+            collective_id=0, has_side_effects=True, vmem_limit_bytes=67043328),
     )(
         inputs.reshape(n, piece, rows),
         weight_first.reshape(half, radix_a, tile, tile),

time: 67.8 us -> 63.6 us (0.938)
  the two profiles are of different devices: /device:TPU:6 before, /device:TPU:0 now
where the time goes in v2:
time: 63.6 us; the launch traced here: 63.5 us
  Pallas kernels  61.8 us (97%)
  local copies, waits for them, and re-layouts  1.67 us (3%)
    pallas_call x1, Pallas kernels, body(): pl.pallas_call(functools.partial(relay, dims), name='relay', out_shape=ja...  61.8 us
    unnamed x1, local copies, waits for them, and re-layouts  1.67 us

profile of v2, /device:TPU:0, one launch (start us, length us, event | category | flops | bytes accessed | tf_op | source)
XLA Modules:
  0.0 63.5 jit_solution(4802992021855515538)
XLA Ops:
  0.0 61.8 %relay.1 = bf16[4,256,128]{2,1,0:T(8,128)(2,1)} custom-call(bf16[4,256,128]{2,1,0:T(8,128)(2,1)} %bitcast.9, bf16[4,16,128,128]{3,2,1,0:T(8,128)(2,1)} %bitcast.6, bf16[4,8,128,128]{3,2,1,0:T(8,128)(2,1)} %bitcast.8, f32[1,1024]{1,0:T(1,128)} %b1_in.1, f32[1,1024]{1,0:T(1,128)} %b2_in.1, s32[8,16]{1,0:T(8,128)} %bitcast.10, s32[8,8]{1,0:T(8,128)} %bitcast.11), custom_call_target="tpu_custom_call" | custom-call | tf_op jit(solution)/shard_map/relay/pallas_call | solution.py:282
  61.8 1.7 %copy.9 = bf16[1,1024,128]{2,1,0:T(8,128)(2,1)} copy(bf16[1,1024,128]{2,1,0:T(8,128)(2,1)} %bitcast.7) | data formatting | bytes 524288

commit v3 on v2

--- a/solution.py
+++ b/solution.py
@@ -13,7 +13,7 @@
 
 
 def relay(dims, x, w1, w2, b1_in, b2_in, l1_in, l2_in, o, b1, b2, l1, l2, raw1, far1, raw2, far2, til1, til2, col1, col2,
-          in_a, in_b, mid, res, acc, s_w, r_w, l_w, s_in, s_a, r_a, s_f, s_b, r_b, s_o, r_o):
+          in_a, in_b, mid, res, acc, s_w, r_w, l_w, s_in, s_a, r_a, s_f, s_b, r_b, s_o, r_o, ready):
     n, sections, span, chunks, tile = dims
     me = lax.axis_index("owners")
     sec = lax.axis_index("section")
@@ -28,11 +28,30 @@
     last = sections - 1
 
     barrier = pltpu.get_barrier_semaphore()
-    for t in range(sections):
+    par = lax.rem(me, span)
+    base = me - par
+    classes = n // span
+
+    def fellow(k):
+        return lax.rem(me + span * k, n)
+
+    def mate(j):
+        return base + lax.rem(par + j, span)
+
+    def greet(sem, w, t):
+        pl.semaphore_signal(sem, inc=1, device_id={"owners": w, "section": t}, device_id_type=MESH)
+
+    near = [fellow(k) for k in range(1, classes)] + [mate(j) for j in range(1, span)]
+
+    @pl.when(sec == 0)
+    def _():
+        for w in near:
+            greet(barrier, w, 0)
+    for t in range(1, sections):
         for w in range(n):
             @pl.when(jnp.logical_or(me != w, sec != t))
             def _():
-                pl.semaphore_signal(barrier, inc=1, device_id={"owners": w, "section": t}, device_id_type=MESH)
+                greet(barrier, w, t)
     pl.semaphore_signal(barrier, inc=1, device_id={"rep": 1 - rep}, device_id_type=MESH)
 
     local = [
@@ -45,18 +64,20 @@
     ]
     for copy in local:
         copy.start()
-    pl.semaphore_wait(barrier, n * sections)
-
-    par = lax.rem(me, span)
-    base = me - par
-    classes = n // span
+    @pl.when(sec == 0)
+    def _():
+        pl.semaphore_wait(barrier, len(near) + 1)
+
+    @pl.when(sec != 0)
+    def _():
+        pl.semaphore_wait(barrier, n * sections)
+
+    @pl.when(sec == 1)
+    def _():
+        for k in range(classes):
+            greet(ready, fellow(k), 0)
+
     bytes_of = in_a.at[0, 0, 0]
-
-    def fellow(k):
-        return lax.rem(me + span * k, n)
-
-    def mate(j):
-        return base + lax.rem(par + j, span)
 
     def send_a(src, slot, h, w, target, sem):
         pltpu.make_async_remote_copy(
@@ -67,12 +88,9 @@
     def done(sem):
         pltpu.make_async_copy(bytes_of, bytes_of, sem).wait()
 
-    def home_targets():
-        return [fellow(k) for k in range(1, classes)] + [mate(j) for j in range(1, span)]
-
     @pl.when(sec == 0)
     def _():
-        for w in home_targets():
+        for w in near:
             for h in range(span):
                 send_a(x, 0, h, w, 0, s_in)
         for h in range(span):
@@ -205,6 +223,10 @@
         if last > 0:
             @pl.when(sec < last)
             def _():
+                if m == 0:
+                    @pl.when(sec == 0)
+                    def _():
+                        pl.semaphore_wait(ready, classes)
                 for k in range(classes - 1, -1, -1):
                     for h in range(span):
                         send_a(res.at[m], m + 1, h, fellow(k), sec + 1, s_a.at[m])
@@ -224,8 +246,8 @@
     weight_copy(w2, far2, 1).wait_recv()
     arrange(far2, til2, l2, (1 - rep) * half, 1)
     for m in range(sections):
-        if m < last:
-            first_layer(m + 1)
+        if m > 0:
+            first_layer(m)
         second_layer(m)
 
     def sent(ref, sem):
@@ -233,7 +255,7 @@
 
     @pl.when(sec == 0)
     def _():
-        for w in home_targets():
+        for w in near:
             for h in range(span):
                 done(s_in.at[h, w])
 
@@ -307,7 +329,7 @@
             dma((span, n)), dma((sections, span, n)), dma((sections + 1, span, n)),
             dma((sections, span, n, max(span - 1, 1))),
             dma((sections, n)), dma((sections, n)),
-            dma((sections,)), dma((1,)),
+            dma((sections,)), dma((1,)), pltpu.SemaphoreType.REGULAR,
         ],
         compiler_params=pltpu.CompilerParams(
             collective_id=0, has_side_effects=True, vmem_limit_bytes=67043328),

time: 63.6 us -> 61.5 us (0.967)
  the two profiles are of different devices: /device:TPU:0 before, /device:TPU:6 now
where the time goes in v3:
time: 61.5 us; the launch traced here: 61.3 us
  Pallas kernels  59.6 us (97%)
  local copies, waits for them, and re-layouts  1.67 us (3%)
    pallas_call x1, Pallas kernels, body(): pl.pallas_call(functools.partial(relay, dims), name='relay', out_shape=ja...  59.6 us
    unnamed x1, local copies, waits for them, and re-layouts  1.67 us

profile of v3, /device:TPU:6, one launch (start us, length us, event | category | flops | bytes accessed | tf_op | source)
XLA Modules:
  0.0 61.3 jit_solution(13765361691853208612)
XLA Ops:
  0.0 59.6 %relay.1 = bf16[4,256,128]{2,1,0:T(8,128)(2,1)} custom-call(bf16[4,256,128]{2,1,0:T(8,128)(2,1)} %bitcast.9, bf16[4,16,128,128]{3,2,1,0:T(8,128)(2,1)} %bitcast.6, bf16[4,8,128,128]{3,2,1,0:T(8,128)(2,1)} %bitcast.8, f32[1,1024]{1,0:T(1,128)} %b1_in.1, f32[1,1024]{1,0:T(1,128)} %b2_in.1, s32[8,16]{1,0:T(8,128)} %bitcast.10, s32[8,8]{1,0:T(8,128)} %bitcast.11), custom_call_target="tpu_custom_call" | custom-call | tf_op jit(solution)/shard_map/relay/pallas_call | solution.py:304
  59.6 1.7 %copy.9 = bf16[1,1024,128]{2,1,0:T(8,128)(2,1)} copy(bf16[1,1024,128]{2,1,0:T(8,128)(2,1)} %bitcast.7) | data formatting | bytes 524288

commit v4 on v3

--- a/solution.py
+++ b/solution.py
@@ -164,7 +164,10 @@
                 for h in range(span):
                     for j in range(1, span):
                         act(forward(m, h, fellow(k), j))
-            if m == 0 and k > 0:
+            if m == last:
+                if m == 0 and k > 0:
+                    pl.when(sec == 0)(go)
+            elif m == 0 and k > 0:
                 go()
             else:
                 pl.when(sec > 0)(go)
@@ -179,7 +182,10 @@
                 def go():
                     for j in range(1, span):
                         forward(m, h, u, j).start()
-                if m == 0 and k > 0:
+                if m == last:
+                    if m == 0 and k > 0:
+                        pl.when(sec == 0)(go)
+                elif m == 0 and k > 0:
                     go()
                 else:
                     pl.when(sec > 0)(go)
@@ -227,9 +233,9 @@
                     @pl.when(sec == 0)
                     def _():
                         pl.semaphore_wait(ready, classes)
-                for k in range(classes - 1, -1, -1):
+                for d in (range(n - 1, -1, -1) if m == last else range(n - span, -1, -span)):
                     for h in range(span):
-                        send_a(res.at[m], m + 1, h, fellow(k), sec + 1, s_a.at[m])
+                        send_a(res.at[m], m + 1, h, lax.rem(me + d, n), sec + 1, s_a.at[m])
 
         @pl.when(sec == last)
         def _():
@@ -274,9 +280,9 @@
         @pl.when(sec < last)
         def _():
             for m in range(sections):
-                for k in range(classes):
+                for d in range(0, n, 1 if m == last else span):
                     for h in range(span):
-                        done(s_a.at[m, h, fellow(k)])
+                        done(s_a.at[m, h, lax.rem(me + d, n)])
             sent(o, r_o.at[0])
 
         @pl.when(sec == last)

time: 61.5 us -> 59.8 us (0.972)
  Pallas kernels: 59.6 us -> 57.9 us
    pallas_call x1, Pallas kernels: 59.6 us -> 57.9 us  [body(): pl.pallas_call(functools.partial(relay, dims), name='relay', out_shape=ja...]
where the time goes in v4:
time: 59.8 us; the launch traced here: 59.6 us
  Pallas kernels  57.9 us (97%)
  local copies, waits for them, and re-layouts  1.67 us (3%)
    pallas_call x1, Pallas kernels, body(): pl.pallas_call(functools.partial(relay, dims), name='relay', out_shape=ja...  57.9 us
    unnamed x1, local copies, waits for them, and re-layouts  1.67 us

profile of v4, /device:TPU:6, one launch (start us, length us, event | category | flops | bytes accessed | tf_op | source)
XLA Modules:
  0.0 59.6 jit_solution(16131899358090352591)
XLA Ops:
  0.0 57.9 %relay.1 = bf16[4,256,128]{2,1,0:T(8,128)(2,1)} custom-call(bf16[4,256,128]{2,1,0:T(8,128)(2,1)} %bitcast.9, bf16[4,16,128,128]{3,2,1,0:T(8,128)(2,1)} %bitcast.6, bf16[4,8,128,128]{3,2,1,0:T(8,128)(2,1)} %bitcast.8, f32[1,1024]{1,0:T(1,128)} %b1_in.1, f32[1,1024]{1,0:T(1,128)} %b2_in.1, s32[8,16]{1,0:T(8,128)} %bitcast.10, s32[8,8]{1,0:T(8,128)} %bitcast.11), custom_call_target="tpu_custom_call" | custom-call | tf_op jit(solution)/shard_map/relay/pallas_call | solution.py:310
  57.9 1.7 %copy.9 = bf16[1,1024,128]{2,1,0:T(8,128)(2,1)} copy(bf16[1,1024,128]{2,1,0:T(8,128)(2,1)} %bitcast.7) | data formatting | bytes 524288
